TPU v7x, 32 devices: a whole 2x2x4 slice. The times are simulated.
32 devices in a mesh: pulse: 4 (over z), tile: 8 (over y, x, core).
Axes of the slice: x: 2, y: 2, z: 4, core: 2. Of those that a mesh axis runs over, the one named last changes fastest.
Arguments:
- echoes: bfloat16 [2, 128, 4, 16384], P(None, 'pulse', None, 'tile'), may hold values from -6 to 6
- replica: bfloat16 [2, 2048], replicated, may hold values from -0.09375 to 0.09375
- steer_phase: float32 [16, 16], replicated, may hold values from -3.140625 to 3.140625
- range_shift: int32 [2, 32], replicated, may hold values from -8 to 7
- merge_phase: float32 [2, 32], replicated, may hold values from -3.140625 to 3.140625
- merge_frac: float32 [2, 32], replicated, may hold values from 0 to 1
- footprint: int32 [4, 128], P('pulse', 'tile'), may hold values from 0 to 7, as said below
- row_slot: int32 [4, 128], P('pulse', 'tile'), may hold values from 0 to 15
- beam_index: int32 [4, 128, 128], P('pulse', 'tile'), may hold values from 0 to 30
- beam_frac: bfloat16 [4, 128, 128], P('pulse', 'tile'), may hold values from 0 to 1
Outputs:
- image: bfloat16 [2, 4, 128, 16384], P(None, None, 'pulse', 'tile')
Inputs may be any that keep to these rules, and one draw needn't show every extreme that they name: `footprint`: of the 16 blocks of one tile and one pulse block, at most 2 fall on any one tile; in every draw one tile receives exactly 2 blocks from every tile and pulse block.
All inputs are finite; a program needn't handle non-finite values.
Results may differ from a plain program's by a relative error of at most 0.018.
Values may be sent and summed in bfloat16 or wider, within the bound.
A program may use at most 128 MiB of HBM per device.

v0:
```python
import functools
import math

import jax
import jax.numpy as jnp
from jax import lax
from jax.experimental import pallas as pl
from jax.experimental.pallas import tpu as pltpu
from jax.sharding import PartitionSpec as P

RBLOCK = 128
CAP = 2
CBLOCK = 256
EDGE = 128
TABROWS = 16


def shifted(value, axis, by):
    count = lax.axis_size(axis)
    pairs = [(i, i + by) for i in range(count) if 0 <= i + by < count]
    return lax.ppermute(value, axis, pairs)


def iota(shape, dim):
    return lax.broadcasted_iota(jnp.int32, shape, dim)


def form_kernel(
    shift_ref, coef_ref, foot_ref, slot_ref,
    own_ref, next_ref, prev_ref, after_ref, replica_ref, steer_ref, index_ref, frac_ref,
    out_ref,
    ext_ref, toep_ref, sub_ref, merged_ref,
):
    range_dev = own_ref.shape[2]
    rows = own_ref.shape[1]
    taps = replica_ref.shape[1]
    window = CBLOCK + taps
    width = sub_ref.shape[1]
    blocks = range_dev // RBLOCK
    bf16 = jnp.bfloat16

    ext_ref[:, :, 0:EDGE] = prev_ref[...]
    ext_ref[:, :, EDGE : EDGE + range_dev] = own_ref[...]
    ext_ref[:, :, EDGE + range_dev : EDGE + 2 * range_dev] = next_ref[...]
    ext_ref[:, :, EDGE + 2 * range_dev :] = after_ref[...]

    for part in range(2):
        line = replica_ref[part : part + 1, :].astype(jnp.float32)
        line = jnp.concatenate([line, jnp.zeros((1, CBLOCK), jnp.float32)], axis=1)
        rolled = pltpu.roll(
            jnp.broadcast_to(line, (CBLOCK, window)), 0, 1, stride=1, stride_axis=0
        )
        if part == 0:
            toep_ref[0:CBLOCK, 0:window] = rolled.astype(bf16)
            toep_ref[CBLOCK:, window:] = rolled.astype(bf16)
        else:
            toep_ref[0:CBLOCK, window:] = rolled.astype(bf16)
            toep_ref[CBLOCK:, 0:window] = (-rolled).astype(bf16)

    r_at = iota((256, 32), 0)
    left = (((r_at >> 2) & 1) * 16 + ((r_at >> 3) & 15) == iota((256, 32), 1)).astype(bf16)
    k_at = iota((32, 256), 1)
    right = ((k_at >> 7) * 16 + ((k_at >> 2) & 15) == iota((32, 256), 0)).astype(bf16)
    spread = jnp.dot(left, steer_ref[...], preferred_element_type=jnp.float32).astype(bf16)
    spread = jnp.dot(spread, right, preferred_element_type=jnp.float32)
    r_all, k_all = iota((256, 256), 0), iota((256, 256), 1)
    same = ((r_all >> 7) == ((k_all >> 6) & 1)) & ((r_all & 3) == (k_all & 3))
    steer = jnp.where(same, spread, 0.0).astype(bf16)

    group = 3

    def compress(at, carry):
        pieces = []
        for step in range(group):
            start = pl.multiple_of((at * group + step) * CBLOCK, CBLOCK)
            pieces.append(
                jnp.concatenate(
                    [ext_ref[0, :, pl.ds(start, window)], ext_ref[1, :, pl.ds(start, window)]],
                    axis=1,
                )
            )
        left_side = jnp.concatenate(pieces, axis=0)
        found = lax.dot_general(
            left_side, toep_ref[...], (((1,), (1,)), ((), ())),
            preferred_element_type=jnp.float32,
        ).astype(bf16)
        for step in range(group):
            start = pl.multiple_of((at * group + step) * CBLOCK, CBLOCK)
            one = found[step * rows : (step + 1) * rows]
            stacked = jnp.concatenate([one[:, :CBLOCK], one[:, CBLOCK:]], axis=0)
            sub = jnp.dot(steer, stacked, preferred_element_type=jnp.float32)
            sub_ref[:, pl.ds(start, CBLOCK)] = sub.astype(bf16).astype(jnp.float32)
        return carry

    lax.fori_loop(0, width // (CBLOCK * group), compress, 0)

    @pl.when(lax.axis_index("tile") == 0)
    def _():
        sub_ref[:, 0:EDGE] = jnp.zeros((256, EDGE), jnp.float32)

    sign = jnp.where(iota((8, width), 0) < 4, -1.0, 1.0).astype(jnp.float32)

    def merge(a, carry):
        totals = [None, None]
        for c in range(2):
            x = sub_ref[pl.ds(pl.multiple_of((c * 16 + a) * 8, 8), 8), :]
            x_up = pltpu.roll(x, width - 1, 1)
            for parity in range(2):
                b = 2 * a + parity
                weight = coef_ref[0, c * 32 + b]
                cosine = coef_ref[1, c * 32 + b]
                sine = coef_ref[2, c * 32 + b]
                y = (1.0 - weight) * x + weight * x_up
                v = cosine * y + (sine * sign) * pltpu.roll(y, 4, 0)
                by = shift_ref[c, b]
                z = pltpu.roll(v, jnp.where(by > 0, width - by, -by), 1)
                z = z[:, EDGE : EDGE + range_dev]
                totals[parity] = z if totals[parity] is None else totals[parity] + z
        merged_ref[pl.ds(pl.multiple_of(a * 16, 16), 16), :] = jnp.concatenate(
            totals, axis=0
        ).astype(bf16)
        return carry

    lax.fori_loop(0, 16, merge, 0)

    order = (k_all == (r_all & 31) * 8 + (r_all >> 5)).astype(bf16)
    if out_ref.shape[0] > blocks:
        out_ref[...] = jnp.zeros(out_ref.shape, bf16)
    tab_row = iota((TABROWS, RBLOCK), 0)
    for f in range(blocks):
        foot = foot_ref[0, f]
        rank = jnp.int32(0)
        for before in range(f):
            rank = rank + (foot_ref[0, before] == foot).astype(jnp.int32)
        slot = foot * CAP + rank
        part = jnp.dot(
            order, merged_ref[:, f * RBLOCK : (f + 1) * RBLOCK],
            preferred_element_type=jnp.float32,
        )
        out_ref[slot, 0:256, :] = part.astype(bf16)
        landing = (slot_ref[0, f] + 1).astype(jnp.float32)
        index_f = index_ref[0, f : f + 1, :].astype(jnp.float32)
        frac_f = frac_ref[0, f : f + 1, :].astype(jnp.float32)
        table = jnp.where(tab_row == 0, index_f, jnp.where(tab_row == 1, frac_f, 0.0))
        table = jnp.where(tab_row == 2, landing, table)
        out_ref[slot, 256 : 256 + TABROWS, :] = table.astype(bf16)


def place_kernel(got_ref, out_ref, left_ref, right_ref):
    slots = got_ref.shape[0]
    beams = out_ref.shape[1]
    spans = out_ref.shape[2] // RBLOCK
    lanes = spans * beams
    mine = lax.axis_index("pulse") * beams
    bf16 = jnp.bfloat16
    lane = iota((RBLOCK, lanes), 1)
    widen = ((lane & (beams - 1)) + mine == iota((RBLOCK, lanes), 0)).astype(bf16)
    where_at = iota((1, lanes), 1) // beams + 1
    child = iota((32, lanes), 0).astype(jnp.float32)

    def prepare(at, carry):
        table = got_ref[at, 256 : 256 + TABROWS, :]
        wide = jnp.dot(table, widen, preferred_element_type=jnp.float32)
        landing = wide[2:3, :]
        index = jnp.where(landing == where_at.astype(jnp.float32), wide[0:1, :], -9.0)
        frac = wide[1:2, :]
        lower = (1.0 - frac).astype(bf16).astype(jnp.float32)
        weight = jnp.where(child == index, lower, 0.0)
        weight = jnp.where(child == index + 1.0, frac, weight)
        start = pl.multiple_of(at * 32, 32)
        left_ref[pl.ds(start, 32), :] = weight.astype(bf16)
        for x in range(8):
            right_ref[pl.ds(start, 32), x * RBLOCK : (x + 1) * RBLOCK] = got_ref[
                at, x * 32 : (x + 1) * 32, :
            ]
        return carry

    lax.fori_loop(0, slots, prepare, 0)
    for half in range(0, lanes, 256):
        result = lax.dot_general(
            left_ref[:, half : half + 256], right_ref[...], (((0,), (0,)), ((), ())),
            preferred_element_type=jnp.float32,
        ).astype(bf16)
        for sub in range(256 // beams):
            w = half // beams + sub
            for x in range(8):
                out_ref[x, :, w * RBLOCK : (w + 1) * RBLOCK] = result[
                    sub * beams : (sub + 1) * beams, x * RBLOCK : (x + 1) * RBLOCK
                ]


def shards(
    echoes, replica, steer_phase, range_shift, merge_phase, merge_frac,
    footprint, row_slot, beam_index, beam_frac,
):
    pulse_count, pol_count, range_dev = echoes.shape[1:]
    rows = pulse_count * pol_count
    taps = replica.shape[1]
    final_beams = beam_index.shape[2]
    tiles = lax.axis_size("tile")
    groups = lax.axis_size("pulse")
    slot_count = tiles * CAP
    own = echoes.reshape(2, rows, range_dev)
    following = shifted(own, "tile", -1)
    before = shifted(own[:, :, range_dev - EDGE :], "tile", 1)
    after = shifted(own[:, :, :EDGE], "tile", -2)

    scale = 1.0 / math.sqrt(steer_phase.shape[1])
    steer_re = jnp.cos(steer_phase) * scale
    steer_im = jnp.sin(steer_phase) * scale
    steer = jnp.concatenate(
        [
            jnp.concatenate([steer_re, -steer_im], axis=1),
            jnp.concatenate([steer_im, steer_re], axis=1),
        ],
        axis=0,
    ).astype(jnp.bfloat16)
    half_root = math.sqrt(0.5)
    coef = jnp.stack(
        [
            merge_frac.reshape(-1),
            (jnp.cos(merge_phase) * half_root).reshape(-1),
            (jnp.sin(merge_phase) * half_root).reshape(-1),
        ]
    )
    width = range_dev + CBLOCK
    smem = pl.BlockSpec(memory_space=pltpu.SMEM)
    vmem = pl.BlockSpec(memory_space=pltpu.VMEM)
    sent = pl.pallas_call(
        form_kernel,
        out_shape=jax.ShapeDtypeStruct((slot_count, 256 + TABROWS, RBLOCK), jnp.bfloat16),
        in_specs=[smem] * 4 + [vmem] * 8,
        out_specs=vmem,
        scratch_shapes=[
            pltpu.VMEM((2, rows, 2 * range_dev + 2 * EDGE), jnp.bfloat16),
            pltpu.VMEM((2 * CBLOCK, 2 * (CBLOCK + taps)), jnp.bfloat16),
            pltpu.VMEM((256, width), jnp.float32),
            pltpu.VMEM((256, range_dev), jnp.bfloat16),
        ],
        compiler_params=pltpu.CompilerParams(vmem_limit_bytes=56 << 20),
    )(
        range_shift, coef, footprint, row_slot,
        own, following, before, after, replica, steer, beam_index, beam_frac,
    )
    got = lax.all_to_all(
        sent.reshape(tiles, CAP, 256 + TABROWS, RBLOCK), "tile",
        split_axis=0, concat_axis=0, tiled=True,
    ).reshape(slot_count, 256 + TABROWS, RBLOCK)
    gathered = lax.all_gather(got, "pulse", axis=0, tiled=True)
    beams = final_beams // groups
    total_slots = groups * slot_count
    image = pl.pallas_call(
        place_kernel,
        out_shape=jax.ShapeDtypeStruct((2 * pol_count, beams, range_dev), jnp.bfloat16),
        in_specs=[vmem],
        out_specs=vmem,
        scratch_shapes=[
            pltpu.VMEM((total_slots * 32, range_dev // RBLOCK * beams), jnp.bfloat16),
            pltpu.VMEM((total_slots * 32, 8 * RBLOCK), jnp.bfloat16),
        ],
        compiler_params=pltpu.CompilerParams(vmem_limit_bytes=56 << 20),
    )(gathered)
    return image.reshape(2, pol_count, beams, range_dev)


def solution(mesh):
    placed = (
        P(None, "pulse", None, "tile"),
        P(),
        P(),
        P(),
        P(),
        P(),
        P("pulse", "tile"),
        P("pulse", "tile"),
        P("pulse", "tile", None),
        P("pulse", "tile", None),
    )
    return jax.shard_map(
        shards,
        mesh=mesh,
        in_specs=placed,
        out_specs=P(None, None, "pulse", "tile"),
        check_vma=False,
    )
```

profile of v0, /device:TPU:0, one launch (start us, length us, event | category | flops | bytes accessed | tf_op | source)
XLA Modules:
  0.0 170.9 jit_solution(4760430635628293156)
XLA Ops:
  6.5 0.0 copy-start.6
  6.5 0.0 copy-start.5
  6.5 0.0 copy-start.4
  6.5 0.0 all-gather.2.cloned.1.call-start
  6.5 1.4 reshape.12.own_ref
  7.9 0.0 copy-start
  7.9 1.3 collective-permute-start
  9.3 1.3 collective-permute-start.2
  10.6 3.0 %collective-permute-start.1 = (bf16[2,128,128]{2,1,0:T(8,128)(2,1)S(1)}, bf16[2,128,128]{2,1,0:T(8,128)(2,1)S(1)}, u32[]{:S(2)}, u32[]{:S(2)}) collective-permute-start(bf16[2,128,128]{2,1,0:T(8,128)(2,1)S(1)} %get-tuple-element.6), channel_id=1, source_target_pairs={{0,1},{1,2},{2,3},{3,4},{4,5},{5,6},{6,7},{8,9},{9,10},{10,11},{11... | collective-permute-start | bytes 196616 | tf_op jit(solution)/shard_map/ppermute | solution.py:21
  13.6 0.0 copy-done.6
  13.6 0.1 stack_reshape.9
  13.7 0.0 copy-done.5
  13.7 0.1 stack_reshape.10
  13.8 0.1 stack_reshape.11
  13.9 0.0 copy-done.4
  13.9 0.1 negate_convert_fusion
  14.0 0.7 maximum_maximum_fusion.steer_ref
  14.6 0.6 pad_maximum_fusion.coef_ref
  15.2 12.4 %collective-permute-done.2.after_ref = bf16[2,128,128]{2,1,0:T(8,128)(2,1)S(1)} collective-permute-done((bf16[2,128,128]{2,1,0:T(8,128)(2,1)S(1)}, bf16[2,128,128]{2,1,0:T(8,128)(2,1)S(1)}, u32[]{:S(2)}, u32[]{:S(2)}) %collective-permute-start.2) | collective-permute-done | bytes 65568 | tf_op jit(solution)/shard_map/ppermute | solution.py:21
  27.7 0.0 copy-start.2
  27.7 0.0 collective-permute-done.1.prev_ref
  27.7 0.0 copy-start.3
  27.7 0.0 collective-permute-done.next_ref
  27.7 0.0 copy-done
  27.7 0.6 copy-done.2
  28.3 0.0 copy-done.3
  28.3 1.0 copy-done.1
  29.3 14.5 %shard_map.100 = bf16[16,272,128]{2,1,0:T(8,128)(2,1)} custom-call(s32[2,32]{1,0:T(2,128)} %shift_ref.1, f32[3,64]{1,0:T(4,128)} %pad_maximum_fusion.coef_ref, s32[1,16]{1,0:T(1,128)} %foot_ref.1, s32[1,16]{1,0:T(1,128)} %slot_ref.1, bf16[2,128,2048]{2,1,0:T(8,128)(2,1)} %copy-done, bf16[2,128,2048]{2,1,0:T(8,128)(2,1)} %copy-done.1, ...), custom_call_target="tpu_custom_call" | custom-call | tf_op jit(solution)/shard_map/pallas_call | solution.py:229
  43.8 20.3 %all_to_all.5 = bf16[8,2,272,128]{3,2,1,0:T(8,128)(2,1)} all-to-all(bf16[8,2,272,128]{3,2,1,0:T(8,128)(2,1)} %bitcast.4), channel_id=1, replica_groups=mesh['pulse'=4,'tile'=8] {'tile'}, dimensions={0} | all-to-all | bytes 2228224 | tf_op jit(solution)/shard_map/all_to_all | solution.py:245
  64.1 0.0 all-gather.2.cloned.1.call-update
  64.1 84.6 %all-gather.2.cloned.1.call-done.got_ref = bf16[64,272,128]{2,1,0:T(8,128)(2,1)} async-done(((bf16[16,272,128]{2,1,0:T(8,128)(2,1)}), bf16[64,272,128]{2,1,0:T(8,128)(2,1)}) %all-gather.2.cloned.1.call-update) | async-done | bytes 4456464 | tf_op jit(solution)/shard_map/all_gather | solution.py:249
  148.8 15.3 %shard_map.101 = bf16[8,32,2048]{2,1,0:T(8,128)(2,1)} custom-call(bf16[64,272,128]{2,1,0:T(8,128)(2,1)} %all-gather.2.cloned.1.call-done.got_ref), custom_call_target="tpu_custom_call" | custom-call | tf_op jit(solution)/shard_map/pallas_call | solution.py:252
  (3 shorter events, 0.1 us)
Async XLA Ops:
  6.5 7.1 %copy-start.6 = (f32[2,32]{1,0:T(2,128)S(1)}, f32[2,32]{1,0:T(2,128)}, u32[]{:S(2)}) copy-start(f32[2,32]{1,0:T(2,128)} %param.15) | copy-start | bytes 772
  6.5 7.2 %copy-start.5 = (f32[2,32]{1,0:T(2,128)S(1)}, f32[2,32]{1,0:T(2,128)}, u32[]{:S(2)}) copy-start(f32[2,32]{1,0:T(2,128)} %param.14) | copy-start | bytes 772
  6.5 7.4 %copy-start.4 = (f32[16,16]{1,0:T(8,128)S(1)}, f32[16,16]{1,0:T(8,128)}, u32[]{:S(2)}) copy-start(f32[16,16]{1,0:T(8,128)} %param.12) | copy-start | bytes 3076
  6.5 142.2 %all-gather.2.cloned.1.call-start = ((), (), s32[]{:S(2)}) async-start(), calls=%async_computation.1 | async-start | bytes 5570560 | tf_op jit(solution)/shard_map/all_gather | solution.py:249
  7.9 19.8 %copy-start = (bf16[2,128,2048]{2,1,0:T(8,128)(2,1)}, bf16[2,128,2048]{2,1,0:T(8,128)(2,1)S(1)}, u32[]{:S(2)}) copy-start(bf16[2,128,2048]{2,1,0:T(8,128)(2,1)S(1)} %reshape.12.own_ref) | copy-start | bytes 3145732
  7.9 19.7 %collective-permute-start = (bf16[2,128,2048]{2,1,0:T(8,128)(2,1)S(1)}, bf16[2,128,2048]{2,1,0:T(8,128)(2,1)S(1)}, u32[]{:S(2)}, u32[]{:S(2)}) collective-permute-start(bf16[2,128,2048]{2,1,0:T(8,128)(2,1)S(1)} %reshape.12.own_ref), channel_id=1, source_target_pairs={{1,0},{2,1},{3,2},{4,3},{5,4},{6,5},{7,6},{9,8},{10,9},{11,10},{12... | collective-permute-start | bytes 3145736 | tf_op jit(solution)/shard_map/ppermute | solution.py:21
  9.3 18.4 %collective-permute-start.2 = (bf16[2,128,128]{2,1,0:T(8,128)(2,1)S(1)}, bf16[2,128,128]{2,1,0:T(8,128)(2,1)S(1)}, u32[]{:S(2)}, u32[]{:S(2)}) collective-permute-start(bf16[2,128,128]{2,1,0:T(8,128)(2,1)S(1)} %get-tuple-element.5), channel_id=1, source_target_pairs={{2,0},{3,1},{4,2},{5,3},{6,4},{7,5},{10,8},{11,9},{12,10},{13,11},... | collective-permute-start | bytes 196616 | tf_op jit(solution)/shard_map/ppermute | solution.py:21
  10.6 17.1 %collective-permute-start.1 = (bf16[2,128,128]{2,1,0:T(8,128)(2,1)S(1)}, bf16[2,128,128]{2,1,0:T(8,128)(2,1)S(1)}, u32[]{:S(2)}, u32[]{:S(2)}) collective-permute-start(bf16[2,128,128]{2,1,0:T(8,128)(2,1)S(1)} %get-tuple-element.6), channel_id=1, source_target_pairs={{0,1},{1,2},{2,3},{3,4},{4,5},{5,6},{6,7},{8,9},{9,10},{10,11},{11... | collective-permute-start | bytes 196616 | tf_op jit(solution)/shard_map/ppermute | solution.py:21
  27.7 0.6 copy-start.2
  27.7 0.6 copy-start.3
  28.3 1.0 copy-start.1
Sparse Core Ops, SparseCore 0:
  64.3 84.4 all-gather.1
where the time goes:
time: 171 us
  waiting for transfers between devices  97.1 us (57%)
  Pallas kernels  29.8 us (17%)
  blocking collectives  20.3 us (12%)
  between operations  13.5 us (8%)
  starting transfers between devices  5.62 us (3%)
  local copies, waits for them, and re-layouts  3.27 us (2%)
    all_gather x1, waiting for transfers between devices, shards(): gathered = lax.all_gather(got, 'pulse', axis=0, tiled=True)  84.6 us
    all_to_all x1, blocking collectives, shards(): lax.all_to_all(sent.reshape(tiles, CAP, 256 + TABROWS, RBLOCK), 'tile', s...  20.3 us
    pallas_call x1, Pallas kernels, shards(): pl.pallas_call(place_kernel, out_shape=jax.ShapeDtypeStruct((2 * pol_coun...  15.3 us
    pallas_call x1, Pallas kernels, shards(): pl.pallas_call(form_kernel, out_shape=jax.ShapeDtypeStruct((slot_count, 2...  14.5 us
    ppermute x3, waiting for transfers between devices, shifted(): return lax.ppermute(value, axis, pairs)  12.4 us
    ppermute x3, starting transfers between devices, shifted(): return lax.ppermute(value, axis, pairs)  5.62 us
  transfers between devices with their start and end apart: 4, of which 2 were waited for; matrix products, arithmetic and copies ran while one was open for 1% of the time, Pallas kernels for 0%

commit v1 on v0

--- a/solution.py
+++ b/solution.py
@@ -28,7 +28,7 @@
 def form_kernel(
     shift_ref, coef_ref, foot_ref, slot_ref,
     own_ref, next_ref, prev_ref, after_ref, replica_ref, steer_ref, index_ref, frac_ref,
-    out_ref,
+    kid_ref, tab_ref,
     ext_ref, toep_ref, sub_ref, merged_ref,
 ):
     range_dev = own_ref.shape[2]
@@ -124,8 +124,9 @@
     lax.fori_loop(0, 16, merge, 0)
 
     order = (k_all == (r_all & 31) * 8 + (r_all >> 5)).astype(bf16)
-    if out_ref.shape[0] > blocks:
-        out_ref[...] = jnp.zeros(out_ref.shape, bf16)
+    if tab_ref.shape[0] > blocks:
+        kid_ref[...] = jnp.zeros(kid_ref.shape, bf16)
+        tab_ref[...] = jnp.zeros(tab_ref.shape, bf16)
     tab_row = iota((TABROWS, RBLOCK), 0)
     for f in range(blocks):
         foot = foot_ref[0, f]
@@ -137,13 +138,13 @@
             order, merged_ref[:, f * RBLOCK : (f + 1) * RBLOCK],
             preferred_element_type=jnp.float32,
         )
-        out_ref[slot, 0:256, :] = part.astype(bf16)
+        kid_ref[:, slot] = part.astype(bf16).reshape(8, 32, RBLOCK)
         landing = (slot_ref[0, f] + 1).astype(jnp.float32)
         index_f = index_ref[0, f : f + 1, :].astype(jnp.float32)
         frac_f = frac_ref[0, f : f + 1, :].astype(jnp.float32)
         table = jnp.where(tab_row == 0, index_f, jnp.where(tab_row == 1, frac_f, 0.0))
         table = jnp.where(tab_row == 2, landing, table)
-        out_ref[slot, 256 : 256 + TABROWS, :] = table.astype(bf16)
+        tab_ref[slot] = table.astype(bf16)
 
 
 def place_kernel(got_ref, out_ref, left_ref, right_ref):
@@ -187,6 +188,240 @@
                 out_ref[x, :, w * RBLOCK : (w + 1) * RBLOCK] = result[
                     sub * beams : (sub + 1) * beams, x * RBLOCK : (x + 1) * RBLOCK
                 ]
+
+
+CHUNKS = 4
+MESH = pl.DeviceIdType.MESH
+
+
+def line_kernel(
+    tiles, kid_ref, tab_ref, out_ref,
+    kids, tabs, left_ref, part_ref, arrived_ref, own_ref,
+    a2a_send, a2a_recv, line_send, line_recv, part_send, part_recv, local_sem,
+):
+    g = lax.axis_index("pulse")
+    t = lax.axis_index("tile")
+    beams = out_ref.shape[1]
+    spans = out_ref.shape[2] // RBLOCK
+    lanes = spans * beams
+    slots = tiles * CAP
+    depth = slots * 32
+    per = 8 // CHUNKS
+    bf16 = jnp.bfloat16
+    f32 = jnp.float32
+    is_mid = (g == 1) | (g == 2)
+    inner = jnp.where(g == 0, 1, jnp.where(g == 1, 2, jnp.where(g == 2, 1, 2)))
+    end = jnp.where(g < 2, 0, 3)
+    far = 3 - end
+
+    barrier = pltpu.get_barrier_semaphore()
+    for d in range(1, tiles):
+        pl.semaphore_signal(
+            barrier, inc=1, device_id={"tile": lax.rem(t + d, tiles)}, device_id_type=MESH
+        )
+    pl.semaphore_signal(barrier, inc=1, device_id={"pulse": inner}, device_id_type=MESH)
+
+    @pl.when(is_mid)
+    def _():
+        pl.semaphore_signal(barrier, inc=1, device_id={"pulse": end}, device_id_type=MESH)
+        pl.semaphore_wait(barrier, tiles + 1)
+
+    @pl.when(jnp.logical_not(is_mid))
+    def _():
+        pl.semaphore_wait(barrier, tiles)
+
+    def spread_copy(k, d, peer, place):
+        if k == CHUNKS:
+            src = tab_ref.at[pl.ds(peer * CAP, CAP)]
+            dst = tabs.at[g, pl.ds(place * CAP, CAP)]
+        else:
+            src = kid_ref.at[pl.ds(k * per, per), pl.ds(peer * CAP, CAP)]
+            dst = kids.at[g, pl.ds(k * per, per), pl.ds(place * CAP, CAP)]
+        return pltpu.make_async_remote_copy(
+            src_ref=src, dst_ref=dst,
+            send_sem=a2a_send.at[k, d - 1], recv_sem=a2a_recv.at[k, d - 1],
+            device_id={"tile": peer}, device_id_type=MESH,
+        )
+
+    order = [CHUNKS] + list(range(CHUNKS))
+    for k in order:
+        for d in range(1, tiles):
+            spread_copy(k, d, lax.rem(t + d, tiles), t).start()
+    keep_tab = pltpu.make_async_copy(
+        tab_ref.at[pl.ds(t * CAP, CAP)], tabs.at[g, pl.ds(t * CAP, CAP)], local_sem.at[0]
+    )
+    keep_kid = pltpu.make_async_copy(
+        kid_ref.at[:, pl.ds(t * CAP, CAP)], kids.at[g, :, pl.ds(t * CAP, CAP)], local_sem.at[1]
+    )
+    keep_tab.start()
+    keep_kid.start()
+    keep_tab.wait()
+    keep_kid.wait()
+
+    def spread_wait(k):
+        for d in range(1, tiles):
+            peer = lax.rem(t + tiles - d, tiles)
+            spread_copy(k, d, peer, peer).wait_recv()
+
+    def line_copy(k, group, lane, to):
+        if k == CHUNKS:
+            part = tabs.at[group]
+        else:
+            part = kids.at[group, pl.ds(k * per, per)]
+        return pltpu.make_async_remote_copy(
+            src_ref=part, dst_ref=part,
+            send_sem=line_send.at[lane, k], recv_sem=line_recv.at[group, k],
+            device_id={"pulse": to}, device_id_type=MESH,
+        )
+
+    def part_copy(k, to):
+        return pltpu.make_async_remote_copy(
+            src_ref=part_ref.at[pl.ds(k * per, per)],
+            dst_ref=arrived_ref.at[pl.ds(k * per, per)],
+            send_sem=part_send.at[k], recv_sem=part_recv.at[k],
+            device_id={"pulse": to}, device_id_type=MESH,
+        )
+
+    def prepare(group, beam_group, row, column, used):
+        expand = (
+            (iota((RBLOCK, lanes), 1) & (beams - 1)) + beam_group * beams
+            == iota((RBLOCK, lanes), 0)
+        ).astype(bf16)
+        where_at = (iota((1, lanes), 1) // beams + 1).astype(f32)
+        child = iota((32, lanes), 0).astype(f32)
+
+        def four(at, carry):
+            pieces = []
+            for step in range(4):
+                wide = jnp.dot(
+                    tabs[group, at * 4 + step], expand, preferred_element_type=f32
+                )
+                index = jnp.where((wide[2:3, :] == where_at) & used, wide[0:1, :], -9.0)
+                frac = wide[1:2, :]
+                lower = (1.0 - frac).astype(bf16).astype(f32)
+                weight = jnp.where(child == index, lower, 0.0)
+                pieces.append(jnp.where(child == index + 1.0, frac, weight))
+            block = jnp.concatenate(pieces, axis=0)
+            at_column = pl.multiple_of(column + at * 128, 128)
+            left_ref[row : row + lanes, pl.ds(at_column, 128)] = block.T.astype(bf16)
+            return carry
+
+        lax.fori_loop(0, slots // 4, four, 0)
+
+    @pl.when(is_mid)
+    def _():
+        def begin(k):
+            spread_wait(k)
+            line_copy(k, g, 0, inner).start()
+            line_copy(k, end, 0, inner).wait_recv()
+            line_copy(k, end, 1, inner).start()
+
+        def finish(k):
+            line_copy(k, inner, 0, inner).wait_recv()
+            line_copy(k, far, 0, inner).wait_recv()
+
+        begin(CHUNKS)
+        begin(0)
+        finish(CHUNKS)
+
+        def prepare_group(group, carry):
+            column = pl.multiple_of(group * depth, 128)
+            prepare(group, g, 0, column, group >= 0)
+            prepare(group, end, lanes, column, group != end)
+            return carry
+
+        lax.fori_loop(0, 4, prepare_group, 0)
+        for k in range(CHUNKS):
+            if k + 1 < CHUNKS:
+                begin(k + 1)
+            finish(k)
+            right = jnp.concatenate(
+                [kids[:, k * per + i].reshape(4 * depth, RBLOCK) for i in range(per)], axis=1
+            )
+            result = jnp.dot(
+                left_ref[lanes:, :], right, preferred_element_type=f32
+            ).astype(bf16)
+            for w in range(spans):
+                for i in range(per):
+                    part_ref[k * per + i, :, w * RBLOCK : (w + 1) * RBLOCK] = result[
+                        w * beams : (w + 1) * beams, i * RBLOCK : (i + 1) * RBLOCK
+                    ]
+            part_copy(k, end).start()
+            result = jnp.dot(
+                left_ref[:lanes, :], right, preferred_element_type=f32
+            ).astype(bf16)
+            for w in range(spans):
+                for i in range(per):
+                    out_ref[k * per + i, :, w * RBLOCK : (w + 1) * RBLOCK] = result[
+                        w * beams : (w + 1) * beams, i * RBLOCK : (i + 1) * RBLOCK
+                    ]
+        for k in order:
+            line_copy(k, g, 0, inner).wait_send()
+            line_copy(k, end, 1, inner).wait_send()
+        for k in range(CHUNKS):
+            part_copy(k, end).wait_send()
+
+    @pl.when(jnp.logical_not(is_mid))
+    def _():
+        for k in order:
+            spread_wait(k)
+            line_copy(k, g, 0, inner).start()
+        prepare(g, g, 0, 0, g >= 0)
+        for k in range(CHUNKS):
+            right = jnp.concatenate(
+                [kids[g, k * per + i].reshape(depth, RBLOCK) for i in range(per)], axis=1
+            )
+            result = jnp.dot(
+                left_ref[:lanes, :depth], right, preferred_element_type=f32
+            )
+            for w in range(spans):
+                for i in range(per):
+                    own_ref[k * per + i, :, w * RBLOCK : (w + 1) * RBLOCK] = result[
+                        w * beams : (w + 1) * beams, i * RBLOCK : (i + 1) * RBLOCK
+                    ]
+        for k in range(CHUNKS):
+            part_copy(k, inner).wait_recv()
+            for i in range(per):
+                x = k * per + i
+                out_ref[x] = (own_ref[x] + arrived_ref[x].astype(f32)).astype(bf16)
+        for k in order:
+            line_copy(k, g, 0, inner).wait_send()
+
+    for k in order:
+        for d in range(1, tiles):
+            spread_copy(k, d, lax.rem(t + d, tiles), t).wait_send()
+
+
+def line_exchange(kids, tabs, tiles, beams, range_dev):
+    slots = tiles * CAP
+    lanes = range_dev // RBLOCK * beams
+    bf16 = jnp.bfloat16
+    vmem = pl.BlockSpec(memory_space=pltpu.VMEM)
+    dma = pltpu.SemaphoreType.DMA
+    return pl.pallas_call(
+        functools.partial(line_kernel, tiles),
+        out_shape=jax.ShapeDtypeStruct((8, beams, range_dev), bf16),
+        in_specs=[vmem, vmem],
+        out_specs=vmem,
+        scratch_shapes=[
+            pltpu.VMEM((4, 8, slots, 32, RBLOCK), bf16),
+            pltpu.VMEM((4, slots, TABROWS, RBLOCK), bf16),
+            pltpu.VMEM((2 * lanes, 4 * slots * 32), bf16),
+            pltpu.VMEM((8, beams, range_dev), bf16),
+            pltpu.VMEM((8, beams, range_dev), bf16),
+            pltpu.VMEM((8, beams, range_dev), jnp.float32),
+            dma((CHUNKS + 1, tiles - 1)),
+            dma((CHUNKS + 1, tiles - 1)),
+            dma((2, CHUNKS + 1)),
+            dma((4, CHUNKS + 1)),
+            dma((CHUNKS,)),
+            dma((CHUNKS,)),
+            dma((2,)),
+        ],
+        compiler_params=pltpu.CompilerParams(
+            collective_id=0, has_side_effects=True, vmem_limit_bytes=56 << 20
+        ),
+    )(kids, tabs)
 
 
 def shards(
@@ -226,11 +461,14 @@
     width = range_dev + CBLOCK
     smem = pl.BlockSpec(memory_space=pltpu.SMEM)
     vmem = pl.BlockSpec(memory_space=pltpu.VMEM)
-    sent = pl.pallas_call(
+    kids, tabs = pl.pallas_call(
         form_kernel,
-        out_shape=jax.ShapeDtypeStruct((slot_count, 256 + TABROWS, RBLOCK), jnp.bfloat16),
+        out_shape=(
+            jax.ShapeDtypeStruct((8, slot_count, 32, RBLOCK), jnp.bfloat16),
+            jax.ShapeDtypeStruct((slot_count, TABROWS, RBLOCK), jnp.bfloat16),
+        ),
         in_specs=[smem] * 4 + [vmem] * 8,
-        out_specs=vmem,
+        out_specs=(vmem, vmem),
         scratch_shapes=[
             pltpu.VMEM((2, rows, 2 * range_dev + 2 * EDGE), jnp.bfloat16),
             pltpu.VMEM((2 * CBLOCK, 2 * (CBLOCK + taps)), jnp.bfloat16),
@@ -242,12 +480,18 @@
         range_shift, coef, footprint, row_slot,
         own, following, before, after, replica, steer, beam_index, beam_frac,
     )
+    beams = final_beams // groups
+    if groups == 4:
+        image = line_exchange(kids, tabs, tiles, beams, range_dev)
+        return image.reshape(2, pol_count, beams, range_dev)
+    sent = jnp.concatenate(
+        [kids.transpose(1, 0, 2, 3).reshape(slot_count, 256, RBLOCK), tabs], axis=1
+    )
     got = lax.all_to_all(
         sent.reshape(tiles, CAP, 256 + TABROWS, RBLOCK), "tile",
         split_axis=0, concat_axis=0, tiled=True,
     ).reshape(slot_count, 256 + TABROWS, RBLOCK)
     gathered = lax.all_gather(got, "pulse", axis=0, tiled=True)
-    beams = final_beams // groups
     total_slots = groups * slot_count
     image = pl.pallas_call(
         place_kernel,

time: 171 us -> 112 us (0.65)
  waiting for transfers between devices: 97.1 us -> 12.4 us
  Pallas kernels: 29.8 us -> 85.8 us
  blocking collectives: 20.3 us -> 0 us
  between operations: 13.5 us -> 0.12 us
  local copies, waits for them, and re-layouts: 3.27 us -> 5.57 us
    all_gather x1 -> x0, waiting for transfers between devices: 84.6 us -> none  [shards(): gathered = lax.all_gather(got, 'pulse', axis=0, tiled=True)]
    pallas_call x2, Pallas kernels: 29.8 us -> 85.8 us  [the longest x1 71.3 us: line_exchange(): pl.pallas_call(functools.partial(line_kernel, tiles), out_shape=jax.Shape...]
    all_to_all x1 -> x0, blocking collectives: 20.3 us -> none  [shards(): lax.all_to_all(sent.reshape(tiles, CAP, 256 + TABROWS, RBLOCK), 'tile', s...]
    unnamed x14 -> x15, local copies, waits for them, and re-layouts: 1.63 us -> 3.96 us
  transfers between devices with their start and end apart: 4 -> 3, of which waited for: 2 -> 1; matrix products, arithmetic and copies ran while one was open for 1% -> 1% of each run, Pallas kernels for 0% -> 0%
where the time goes in v1:
time: 112 us; the launch traced here: 111 us
  Pallas kernels  85.8 us (77%)
  waiting for transfers between devices  12.4 us (11%)
  starting transfers between devices  5.62 us (5%)
  local copies, waits for them, and re-layouts  5.57 us (5%)
  other arithmetic  1.3 us (1%)
    pallas_call x1, Pallas kernels, line_exchange(): pl.pallas_call(functools.partial(line_kernel, tiles), out_shape=jax.Shape...  71.3 us
    pallas_call x1, Pallas kernels, shards(): pl.pallas_call(form_kernel, out_shape=(jax.ShapeDtypeStruct((8, slot_coun...  14.5 us
    ppermute x3, waiting for transfers between devices, shifted(): return lax.ppermute(value, axis, pairs)  12.4 us
    ppermute x3, starting transfers between devices, shifted(): return lax.ppermute(value, axis, pairs)  5.62 us
    unnamed x15, local copies, waits for them, and re-layouts  3.96 us
  transfers between devices with their start and end apart: 3, of which 1 were waited for; matrix products, arithmetic and copies ran while one was open for 1% of the time, Pallas kernels for 0%

profile of v1, /device:TPU:0, one launch (start us, length us, event | category | flops | bytes accessed | tf_op | source)
XLA Modules:
  0.0 110.8 jit_solution(15778102434203729999)
XLA Ops:
  0.0 1.3 %reshape.6.own_ref = bf16[2,128,2048]{2,1,0:T(8,128)(2,1)S(1)} reshape(bf16[2,32,4,2048]{3,2,1,0:T(4,128)(2,1)} %param.10) | data formatting | bytes 2097152 | tf_op jit(solution)/shard_map/reshape | solution.py:438
  1.3 0.0 copy-start
  1.4 1.3 %collective-permute-start = (bf16[2,128,2048]{2,1,0:T(8,128)(2,1)S(1)}, bf16[2,128,2048]{2,1,0:T(8,128)(2,1)S(1)}, u32[]{:S(2)}, u32[]{:S(2)}) collective-permute-start(bf16[2,128,2048]{2,1,0:T(8,128)(2,1)S(1)} %reshape.6.own_ref), channel_id=1, source_target_pairs={{1,0},{2,1},{3,2},{4,3},{5,4},{6,5},{7,6},{9,8},{10,9},{11,10},{12... | collective-permute-start | bytes 3145736 | tf_op jit(solution)/shard_map/ppermute | solution.py:21
  2.7 0.0 copy-start.6
  2.7 0.0 copy-start.5
  2.7 0.0 copy-start.4
  2.7 1.3 %collective-permute-start.2 = (bf16[2,128,128]{2,1,0:T(8,128)(2,1)S(1)}, bf16[2,128,128]{2,1,0:T(8,128)(2,1)S(1)}, u32[]{:S(2)}, u32[]{:S(2)}) collective-permute-start(bf16[2,128,128]{2,1,0:T(8,128)(2,1)S(1)} %get-tuple-element.9), channel_id=1, source_target_pairs={{2,0},{3,1},{4,2},{5,3},{6,4},{7,5},{10,8},{11,9},{12,10},{13,11},... | collective-permute-start | bytes 196616 | tf_op jit(solution)/shard_map/ppermute | solution.py:21
  4.0 3.0 %collective-permute-start.1 = (bf16[2,128,128]{2,1,0:T(8,128)(2,1)S(1)}, bf16[2,128,128]{2,1,0:T(8,128)(2,1)S(1)}, u32[]{:S(2)}, u32[]{:S(2)}) collective-permute-start(bf16[2,128,128]{2,1,0:T(8,128)(2,1)S(1)} %get-tuple-element.10), channel_id=1, source_target_pairs={{0,1},{1,2},{2,3},{3,4},{4,5},{5,6},{6,7},{8,9},{9,10},{10,11},{11... | collective-permute-start | bytes 196616 | tf_op jit(solution)/shard_map/ppermute | solution.py:21
  7.1 0.0 copy-done.6
  7.1 0.1 stack_reshape.9
  7.2 0.0 copy-done.5
  7.2 0.1 stack_reshape.10
  7.3 0.1 stack_reshape.11
  7.4 0.0 copy-done.4
  7.4 0.1 negate_convert_fusion
  7.4 0.7 maximum_maximum_fusion.steer_ref
  8.1 0.6 pad_maximum_fusion.coef_ref
  8.6 12.4 %collective-permute-done.2.after_ref = bf16[2,128,128]{2,1,0:T(8,128)(2,1)S(1)} collective-permute-done((bf16[2,128,128]{2,1,0:T(8,128)(2,1)S(1)}, bf16[2,128,128]{2,1,0:T(8,128)(2,1)S(1)}, u32[]{:S(2)}, u32[]{:S(2)}) %collective-permute-start.2) | collective-permute-done | bytes 65568 | tf_op jit(solution)/shard_map/ppermute | solution.py:21
  21.1 0.0 copy-start.2
  21.1 0.0 collective-permute-done.1.prev_ref
  21.1 0.0 copy-start.3
  21.1 0.0 collective-permute-done.next_ref
  21.1 0.0 copy-done
  21.1 0.6 copy-done.2
  21.7 0.0 copy-done.3
  21.7 0.0 copy-start.1
  21.7 1.0 copy-done.1
  22.7 14.5 %shard_map.100 = (bf16[8,16,32,128]{3,2,1,0:T(8,128)(2,1)}, bf16[16,16,128]{2,1,0:T(8,128)(2,1)}) custom-call(s32[2,32]{1,0:T(2,128)} %shift_ref.1, f32[3,64]{1,0:T(4,128)} %pad_maximum_fusion.coef_ref, s32[1,16]{1,0:T(1,128)} %foot_ref.1, s32[1,16]{1,0:T(1,128)} %slot_ref.1, bf16[2,128,2048]{2,1,0:T(8,128)(2,1)} %copy-done, ...), custom_call_target="tpu_custom_call" | custom-call | tf_op jit(solution)/shard_map/pallas_call | solution.py:464
  37.2 71.3 %shard_map.101 = bf16[8,32,2048]{2,1,0:T(8,128)(2,1)} custom-call(bf16[8,16,32,128]{3,2,1,0:T(8,128)(2,1)} %get-tuple-element.7.kid_ref, bf16[16,16,128]{2,1,0:T(8,128)(2,1)} %get-tuple-element.8.tab_ref), custom_call_target="tpu_custom_call" | custom-call | tf_op jit(solution)/shard_map/pallas_call | solution.py:401
  108.5 2.3 %copy.12 = bf16[2,4,32,2048]{3,2,1,0:T(8,128)(2,1)} copy(bf16[2,4,32,2048]{3,2,1,0:T(8,128)(2,1)} %bitcast.1) | data formatting | bytes 2097152
  (2 shorter events, 0.1 us)
Async XLA Ops:
  1.3 19.8 %copy-start = (bf16[2,128,2048]{2,1,0:T(8,128)(2,1)}, bf16[2,128,2048]{2,1,0:T(8,128)(2,1)S(1)}, u32[]{:S(2)}) copy-start(bf16[2,128,2048]{2,1,0:T(8,128)(2,1)S(1)} %reshape.6.own_ref) | copy-start | bytes 3145732
  1.4 19.7 %collective-permute-start = (bf16[2,128,2048]{2,1,0:T(8,128)(2,1)S(1)}, bf16[2,128,2048]{2,1,0:T(8,128)(2,1)S(1)}, u32[]{:S(2)}, u32[]{:S(2)}) collective-permute-start(bf16[2,128,2048]{2,1,0:T(8,128)(2,1)S(1)} %reshape.6.own_ref), channel_id=1, source_target_pairs={{1,0},{2,1},{3,2},{4,3},{5,4},{6,5},{7,6},{9,8},{10,9},{11,10},{12... | collective-permute-start | bytes 3145736 | tf_op jit(solution)/shard_map/ppermute | solution.py:21
  2.7 4.4 %copy-start.6 = (f32[2,32]{1,0:T(2,128)S(1)}, f32[2,32]{1,0:T(2,128)}, u32[]{:S(2)}) copy-start(f32[2,32]{1,0:T(2,128)} %param.15) | copy-start | bytes 772
  2.7 4.5 %copy-start.5 = (f32[2,32]{1,0:T(2,128)S(1)}, f32[2,32]{1,0:T(2,128)}, u32[]{:S(2)}) copy-start(f32[2,32]{1,0:T(2,128)} %param.14) | copy-start | bytes 772
  2.7 4.7 %copy-start.4 = (f32[16,16]{1,0:T(8,128)S(1)}, f32[16,16]{1,0:T(8,128)}, u32[]{:S(2)}) copy-start(f32[16,16]{1,0:T(8,128)} %param.12) | copy-start | bytes 3076
  2.7 18.4 %collective-permute-start.2 = (bf16[2,128,128]{2,1,0:T(8,128)(2,1)S(1)}, bf16[2,128,128]{2,1,0:T(8,128)(2,1)S(1)}, u32[]{:S(2)}, u32[]{:S(2)}) collective-permute-start(bf16[2,128,128]{2,1,0:T(8,128)(2,1)S(1)} %get-tuple-element.9), channel_id=1, source_target_pairs={{2,0},{3,1},{4,2},{5,3},{6,4},{7,5},{10,8},{11,9},{12,10},{13,11},... | collective-permute-start | bytes 196616 | tf_op jit(solution)/shard_map/ppermute | solution.py:21
  4.0 17.1 %collective-permute-start.1 = (bf16[2,128,128]{2,1,0:T(8,128)(2,1)S(1)}, bf16[2,128,128]{2,1,0:T(8,128)(2,1)S(1)}, u32[]{:S(2)}, u32[]{:S(2)}) collective-permute-start(bf16[2,128,128]{2,1,0:T(8,128)(2,1)S(1)} %get-tuple-element.10), channel_id=1, source_target_pairs={{0,1},{1,2},{2,3},{3,4},{4,5},{5,6},{6,7},{8,9},{9,10},{10,11},{11... | collective-permute-start | bytes 196616 | tf_op jit(solution)/shard_map/ppermute | solution.py:21
  21.1 0.6 copy-start.2
  21.1 0.6 copy-start.3
  21.7 1.0 copy-start.1

commit v2 on v1

--- a/solution.py
+++ b/solution.py
@@ -194,10 +194,16 @@
 MESH = pl.DeviceIdType.MESH
 
 
-def line_kernel(
-    tiles, kid_ref, tab_ref, out_ref,
+STAGES = 2
+
+
+def fused_kernel(
+    tiles, shift_ref, coef_ref, foot_ref,
+    echo_ref, replica_ref, steer_ref, table_ref, out_ref,
+    ext_ref, toep_ref, sub_ref, merged_ref, block_ref, kid_ref, tab_ref,
     kids, tabs, left_ref, part_ref, arrived_ref, own_ref,
-    a2a_send, a2a_recv, line_send, line_recv, part_send, part_recv, local_sem,
+    halo_send, halo_recv,
+    a2a_send, a2a_recv, line_send, line_recv, part_send, part_recv,
 ):
     g = lax.axis_index("pulse")
     t = lax.axis_index("tile")
@@ -230,6 +236,169 @@
     def _():
         pl.semaphore_wait(barrier, tiles)
 
+    range_dev = echo_ref.shape[3]
+    rows = echo_ref.shape[2]
+    taps = replica_ref.shape[1]
+    window = CBLOCK + taps
+    width = sub_ref.shape[1]
+    blocks = range_dev // RBLOCK
+
+    halos = [
+        ((0, range_dev), EDGE + range_dev, -1),
+        ((range_dev - EDGE, EDGE), 0, 1),
+        ((0, EDGE), EDGE + 2 * range_dev, -2),
+    ]
+
+    def halo_copy(stage, j):
+        (first, count), to, by = halos[j]
+        return pltpu.make_async_remote_copy(
+            src_ref=echo_ref.at[stage, :, :, pl.ds(first, count)],
+            dst_ref=ext_ref.at[stage, :, :, pl.ds(to, count)],
+            send_sem=halo_send.at[stage, j], recv_sem=halo_recv.at[stage, j],
+            device_id={"tile": lax.rem(t + by + tiles, tiles)}, device_id_type=MESH,
+        )
+
+    def sends(j):
+        by = halos[j][2]
+        return (t + by >= 0) & (t + by < tiles)
+
+    def gets(j):
+        by = halos[j][2]
+        return (t - by >= 0) & (t - by < tiles)
+
+    for stage in range(STAGES):
+        for j in range(3):
+            @pl.when(sends(j))
+            def _():
+                halo_copy(stage, j).start()
+
+    for stage in range(STAGES):
+        for j in range(3):
+            (_, count), to, _ = halos[j]
+
+            @pl.when(jnp.logical_not(gets(j)))
+            def _():
+                ext_ref[stage, :, :, to : to + count] = jnp.zeros((2, rows, count), bf16)
+
+        ext_ref[stage, :, :, EDGE : EDGE + range_dev] = echo_ref[stage]
+
+    for part in range(2):
+        line = replica_ref[part : part + 1, :].astype(f32)
+        line = jnp.concatenate([line, jnp.zeros((1, CBLOCK), f32)], axis=1)
+        rolled = pltpu.roll(
+            jnp.broadcast_to(line, (CBLOCK, window)), 0, 1, stride=1, stride_axis=0
+        )
+        if part == 0:
+            toep_ref[0:CBLOCK, 0:window] = rolled.astype(bf16)
+            toep_ref[CBLOCK:, window:] = rolled.astype(bf16)
+        else:
+            toep_ref[0:CBLOCK, window:] = rolled.astype(bf16)
+            toep_ref[CBLOCK:, 0:window] = (-rolled).astype(bf16)
+
+    r_at = iota((256, 32), 0)
+    turn, want = (r_at >> 2) & 1, (r_at >> 1) & 1
+    picked = jnp.where(turn == 1, 1 - want, want)
+    left = ((picked * 16 + ((r_at >> 3) & 15)) == iota((256, 32), 1)).astype(f32)
+    left = jnp.where((turn == 1) & (want == 0), -left, left).astype(bf16)
+    k_at = iota((32, 128), 1)
+    right = ((k_at >> 6) * 16 + ((k_at >> 1) & 15) == iota((32, 128), 0)).astype(bf16)
+    spread = jnp.dot(left, steer_ref[...], preferred_element_type=f32).astype(bf16)
+    spread = jnp.dot(spread, right, preferred_element_type=f32)
+    r_all, k_all = iota((256, 128), 0), iota((256, 128), 1)
+    same = ((r_all >> 7) == ((k_all >> 5) & 1)) & ((r_all & 1) == (k_all & 1))
+    steer = jnp.where(same, spread, 0.0).astype(bf16)
+    o_all, i_all = iota((128, 128), 0), iota((128, 128), 1)
+    order_in = (o_all & 31) * 4 + ((o_all >> 5) & 1) * 2 + (o_all >> 6)
+    reorder = (i_all == order_in).astype(bf16)
+
+    targets = []
+    for f in range(blocks):
+        rank = jnp.int32(0)
+        for earlier in range(f):
+            rank = rank + (foot_ref[0, earlier] == foot_ref[0, f]).astype(jnp.int32)
+        targets.append(foot_ref[0, f] * CAP + rank)
+    sources = []
+    for s in range(slots):
+        source = jnp.int32(0)
+        for f in range(blocks):
+            source = source + f * (targets[f] == s).astype(jnp.int32)
+        sources.append(source)
+    for s in range(slots):
+        tab_ref[s] = table_ref[sources[s]]
+
+    group = 3
+
+    def form(stage, between):
+        for j in range(3):
+            @pl.when(gets(j))
+            def _():
+                halo_copy(stage, j).wait_recv()
+
+        def compress(at, carry):
+            pieces = []
+            for step in range(group):
+                start = pl.multiple_of((at * group + step) * CBLOCK, CBLOCK)
+                pieces.append(
+                    jnp.concatenate(
+                        [
+                            ext_ref[stage, 0, :, pl.ds(start, window)],
+                            ext_ref[stage, 1, :, pl.ds(start, window)],
+                        ],
+                        axis=1,
+                    )
+                )
+            found = lax.dot_general(
+                jnp.concatenate(pieces, axis=0), toep_ref[...], (((1,), (1,)), ((), ())),
+                preferred_element_type=f32,
+            ).astype(bf16)
+            for step in range(group):
+                start = pl.multiple_of((at * group + step) * CBLOCK, CBLOCK)
+                one = found[step * rows : (step + 1) * rows]
+                stacked = jnp.concatenate([one[:, :CBLOCK], one[:, CBLOCK:]], axis=0)
+                sub = jnp.dot(steer, stacked, preferred_element_type=f32)
+                sub_ref[:, pl.ds(start, CBLOCK)] = sub.astype(bf16).astype(f32)
+            return carry
+
+        lax.fori_loop(0, width // (CBLOCK * group), compress, 0)
+
+        @pl.when(t == 0)
+        def _():
+            sub_ref[:, 0:EDGE] = jnp.zeros((256, EDGE), f32)
+
+        between()
+
+        def merge(a, carry):
+            totals = [None, None]
+            for c in range(2):
+                x = sub_ref[pl.ds(pl.multiple_of((c * 16 + a) * 8, 8), 8), :]
+                x_up = pltpu.roll(x, width - 1, 1)
+                for parity in range(2):
+                    b = 2 * a + parity
+                    weight = coef_ref[0, c * 32 + b]
+                    cosine = coef_ref[1, c * 32 + b]
+                    sine = coef_ref[2, c * 32 + b]
+                    y = (1.0 - weight) * x + weight * x_up
+                    v = cosine * y + sine * pltpu.roll(y, 4, 0)
+                    by = shift_ref[c, b]
+                    z = pltpu.roll(v, jnp.where(by > 0, width - by, -by), 1)
+                    z = z[:, EDGE : EDGE + range_dev]
+                    totals[parity] = z if totals[parity] is None else totals[parity] + z
+            both = jnp.where(
+                iota((8, range_dev), 0) < 4, totals[0], pltpu.roll(totals[1], 4, 0)
+            )
+            merged_ref[pl.ds(pl.multiple_of(a * 8, 8), 8), :] = both
+            return carry
+
+        lax.fori_loop(0, 16, merge, 0)
+        for f in range(blocks):
+            part = jnp.dot(
+                reorder, merged_ref[:, f * RBLOCK : (f + 1) * RBLOCK].astype(bf16),
+                preferred_element_type=f32,
+            )
+            block_ref[f] = part.astype(bf16).reshape(4, 32, RBLOCK)
+        for s in range(slots):
+            kid_ref[stage * 4 : stage * 4 + 4, s] = block_ref[sources[s]]
+
     def spread_copy(k, d, peer, place):
         if k == CHUNKS:
             src = tab_ref.at[pl.ds(peer * CAP, CAP)]
@@ -244,19 +413,10 @@
         )
 
     order = [CHUNKS] + list(range(CHUNKS))
-    for k in order:
+
+    def spread_start(k):
         for d in range(1, tiles):
             spread_copy(k, d, lax.rem(t + d, tiles), t).start()
-    keep_tab = pltpu.make_async_copy(
-        tab_ref.at[pl.ds(t * CAP, CAP)], tabs.at[g, pl.ds(t * CAP, CAP)], local_sem.at[0]
-    )
-    keep_kid = pltpu.make_async_copy(
-        kid_ref.at[:, pl.ds(t * CAP, CAP)], kids.at[g, :, pl.ds(t * CAP, CAP)], local_sem.at[1]
-    )
-    keep_tab.start()
-    keep_kid.start()
-    keep_tab.wait()
-    keep_kid.wait()
 
     def spread_wait(k):
         for d in range(1, tiles):
@@ -308,11 +468,36 @@
 
         lax.fori_loop(0, slots // 4, four, 0)
 
+    def keep(k):
+        if k == CHUNKS:
+            tabs[g, pl.ds(t * CAP, CAP)] = tab_ref[pl.ds(t * CAP, CAP)]
+        else:
+            span = slice(k * per, (k + 1) * per)
+            kids[g, span, pl.ds(t * CAP, CAP)] = kid_ref[span, pl.ds(t * CAP, CAP)]
+
+    def begin_own(k):
+        spread_wait(k)
+        line_copy(k, g, 0, inner).start()
+
+    spread_start(CHUNKS)
+    keep(CHUNKS)
+    form(0, lambda: begin_own(CHUNKS))
+    for k in (0, 1):
+        spread_start(k)
+        keep(k)
+
+    def between():
+        begin_own(0)
+        begin_own(1)
+
+    form(1, between)
+    for k in (2, 3):
+        spread_start(k)
+        keep(k)
+
     @pl.when(is_mid)
     def _():
-        def begin(k):
-            spread_wait(k)
-            line_copy(k, g, 0, inner).start()
+        def relay(k):
             line_copy(k, end, 0, inner).wait_recv()
             line_copy(k, end, 1, inner).start()
 
@@ -320,8 +505,8 @@
             line_copy(k, inner, 0, inner).wait_recv()
             line_copy(k, far, 0, inner).wait_recv()
 
-        begin(CHUNKS)
-        begin(0)
+        relay(CHUNKS)
+        relay(0)
         finish(CHUNKS)
 
         def prepare_group(group, carry):
@@ -331,9 +516,12 @@
             return carry
 
         lax.fori_loop(0, 4, prepare_group, 0)
+        relay(1)
+        begin_own(2)
+        begin_own(3)
         for k in range(CHUNKS):
-            if k + 1 < CHUNKS:
-                begin(k + 1)
+            if 2 <= k + 1 < CHUNKS:
+                relay(k + 1)
             finish(k)
             right = jnp.concatenate(
                 [kids[:, k * per + i].reshape(4 * depth, RBLOCK) for i in range(per)], axis=1
@@ -352,7 +540,7 @@
             ).astype(bf16)
             for w in range(spans):
                 for i in range(per):
-                    out_ref[k * per + i, :, w * RBLOCK : (w + 1) * RBLOCK] = result[
+                    out_ref[i * 4 + k, :, w * RBLOCK : (w + 1) * RBLOCK] = result[
                         w * beams : (w + 1) * beams, i * RBLOCK : (i + 1) * RBLOCK
                     ]
         for k in order:
@@ -363,9 +551,8 @@
 
     @pl.when(jnp.logical_not(is_mid))
     def _():
-        for k in order:
-            spread_wait(k)
-            line_copy(k, g, 0, inner).start()
+        begin_own(2)
+        begin_own(3)
         prepare(g, g, 0, 0, g >= 0)
         for k in range(CHUNKS):
             right = jnp.concatenate(
@@ -383,45 +570,59 @@
             part_copy(k, inner).wait_recv()
             for i in range(per):
                 x = k * per + i
-                out_ref[x] = (own_ref[x] + arrived_ref[x].astype(f32)).astype(bf16)
+                out_ref[i * 4 + k] = (own_ref[x] + arrived_ref[x].astype(f32)).astype(bf16)
         for k in order:
             line_copy(k, g, 0, inner).wait_send()
 
     for k in order:
         for d in range(1, tiles):
             spread_copy(k, d, lax.rem(t + d, tiles), t).wait_send()
-
-
-def line_exchange(kids, tabs, tiles, beams, range_dev):
+    for stage in range(STAGES):
+        for j in range(3):
+            @pl.when(sends(j))
+            def _():
+                halo_copy(stage, j).wait_send()
+
+
+def fused(shift, coef, foot, echoes, replica, steer, tables, tiles, beams, range_dev):
     slots = tiles * CAP
     lanes = range_dev // RBLOCK * beams
     bf16 = jnp.bfloat16
     vmem = pl.BlockSpec(memory_space=pltpu.VMEM)
+    smem = pl.BlockSpec(memory_space=pltpu.SMEM)
     dma = pltpu.SemaphoreType.DMA
     return pl.pallas_call(
-        functools.partial(line_kernel, tiles),
+        functools.partial(fused_kernel, tiles),
         out_shape=jax.ShapeDtypeStruct((8, beams, range_dev), bf16),
-        in_specs=[vmem, vmem],
+        in_specs=[smem] * 3 + [vmem] * 4,
         out_specs=vmem,
         scratch_shapes=[
+            pltpu.VMEM(echoes.shape[:3] + (2 * range_dev + 2 * EDGE,), bf16),
+            pltpu.VMEM((2 * CBLOCK, 2 * (CBLOCK + replica.shape[1])), bf16),
+            pltpu.VMEM((256, range_dev + CBLOCK), jnp.float32),
+            pltpu.VMEM((128, range_dev), jnp.float32),
+            pltpu.VMEM((slots, 4, 32, RBLOCK), bf16),
+            pltpu.VMEM((8, slots, 32, RBLOCK), bf16),
+            pltpu.VMEM((slots, TABROWS, RBLOCK), bf16),
             pltpu.VMEM((4, 8, slots, 32, RBLOCK), bf16),
             pltpu.VMEM((4, slots, TABROWS, RBLOCK), bf16),
             pltpu.VMEM((2 * lanes, 4 * slots * 32), bf16),
             pltpu.VMEM((8, beams, range_dev), bf16),
             pltpu.VMEM((8, beams, range_dev), bf16),
             pltpu.VMEM((8, beams, range_dev), jnp.float32),
+            dma((STAGES, 3)),
+            dma((STAGES, 3)),
             dma((CHUNKS + 1, tiles - 1)),
             dma((CHUNKS + 1, tiles - 1)),
             dma((2, CHUNKS + 1)),
             dma((4, CHUNKS + 1)),
             dma((CHUNKS,)),
             dma((CHUNKS,)),
-            dma((2,)),
         ],
         compiler_params=pltpu.CompilerParams(
             collective_id=0, has_side_effects=True, vmem_limit_bytes=56 << 20
         ),
-    )(kids, tabs)
+    )(shift, coef, foot, echoes, replica, steer, tables)
 
 
 def shards(
@@ -435,11 +636,6 @@
     tiles = lax.axis_size("tile")
     groups = lax.axis_size("pulse")
     slot_count = tiles * CAP
-    own = echoes.reshape(2, rows, range_dev)
-    following = shifted(own, "tile", -1)
-    before = shifted(own[:, :, range_dev - EDGE :], "tile", 1)
-    after = shifted(own[:, :, :EDGE], "tile", -2)
-
     scale = 1.0 / math.sqrt(steer_phase.shape[1])
     steer_re = jnp.cos(steer_phase) * scale
     steer_im = jnp.sin(steer_phase) * scale
@@ -458,6 +654,26 @@
             (jnp.sin(merge_phase) * half_root).reshape(-1),
         ]
     )
+    beams = final_beams // groups
+    if groups == 4 and slot_count == range_dev // RBLOCK:
+        split = echoes.reshape(2, pulse_count, STAGES, pol_count // STAGES, range_dev)
+        split = split.transpose(2, 0, 1, 3, 4).reshape(STAGES, 2, rows // STAGES, range_dev)
+        landing = jnp.broadcast_to(row_slot[0][:, None] + 1, beam_index.shape[1:])
+        tables = jnp.stack(
+            [beam_index[0].astype(jnp.float32), beam_frac[0].astype(jnp.float32),
+             landing.astype(jnp.float32)], axis=1,
+        )
+        tables = jnp.pad(tables, ((0, 0), (0, TABROWS - 3), (0, 0))).astype(jnp.bfloat16)
+        image = fused(
+            range_shift, coef, footprint, split, replica, steer, tables,
+            tiles, beams, range_dev,
+        )
+        return image.reshape(2, pol_count, beams, range_dev)
+    own = echoes.reshape(2, rows, range_dev)
+    following = shifted(own, "tile", -1)
+    before = shifted(own[:, :, range_dev - EDGE :], "tile", 1)
+    after = shifted(own[:, :, :EDGE], "tile", -2)
+
     width = range_dev + CBLOCK
     smem = pl.BlockSpec(memory_space=pltpu.SMEM)
     vmem = pl.BlockSpec(memory_space=pltpu.VMEM)
@@ -480,10 +696,6 @@
         range_shift, coef, footprint, row_slot,
         own, following, before, after, replica, steer, beam_index, beam_frac,
     )
-    beams = final_beams // groups
-    if groups == 4:
-        image = line_exchange(kids, tabs, tiles, beams, range_dev)
-        return image.reshape(2, pol_count, beams, range_dev)
     sent = jnp.concatenate(
         [kids.transpose(1, 0, 2, 3).reshape(slot_count, 256, RBLOCK), tabs], axis=1
     )

time: 112 us -> 108 us (0.964)
  waiting for transfers between devices: 12.4 us -> 0 us
  Pallas kernels: 85.8 us -> 95.4 us
  starting transfers between devices: 5.62 us -> 0 us
  local copies, waits for them, and re-layouts: 5.57 us -> 9.8 us
    ppermute x3 -> x0, waiting for transfers between devices: 12.4 us -> none  [shifted(): return lax.ppermute(value, axis, pairs)]
    pallas_call x2 -> x1, Pallas kernels: 85.8 us -> 95.4 us  [fused(): pl.pallas_call(functools.partial(fused_kernel, tiles), out_shape=jax.Shap...]
    ppermute x3 -> x0, starting transfers between devices: 5.62 us -> none  [shifted(): return lax.ppermute(value, axis, pairs)]
    reshape x1 -> x3, local copies, waits for them, and re-layouts: 1.33 us -> 4.59 us  [the longest x2 3.37 us: shards(): echoes.reshape(2, pulse_count, STAGES, pol_count // STAGES, range_dev)]
    unnamed x15 -> x13, local copies, waits for them, and re-layouts: 3.96 us -> 4.87 us
  transfers between devices with their start and end apart: 3 -> 0, of which waited for: 1 -> 0; matrix products, arithmetic and copies ran while one was open for 1% -> 0% of each run, Pallas kernels for 0% -> 0%
where the time goes in v2:
time: 108 us; the launch traced here: 107 us
  Pallas kernels  95.4 us (88%)
  local copies, waits for them, and re-layouts  9.8 us (9%)
  other arithmetic  2.04 us (2%)
    pallas_call x1, Pallas kernels, fused(): pl.pallas_call(functools.partial(fused_kernel, tiles), out_shape=jax.Shap...  95.4 us
    unnamed x13, local copies, waits for them, and re-layouts  4.87 us
    reshape x2, local copies, waits for them, and re-layouts, shards(): echoes.reshape(2, pulse_count, STAGES, pol_count // STAGES, range_dev)  3.37 us

profile of v2, /device:TPU:0, one launch (start us, length us, event | category | flops | bytes accessed | tf_op | source)
XLA Modules:
  0.0 107.3 jit_solution(1228343340576791323)
XLA Ops:
  0.0 0.0 copy-start.4
  0.0 0.7 copy-done.4
  0.7 0.0 copy-start.5
  0.7 0.0 copy-start.3
  0.7 0.1 stack_reshape.9
  0.8 0.6 copy-done.5
  1.3 0.0 copy-start
  1.3 0.0 copy-done.3
  1.4 0.1 stack_reshape.10
  1.5 0.1 stack_reshape.11
  1.6 0.6 pad_maximum_fusion.coef_ref
  2.2 0.0 copy-done
  2.2 0.0 copy-start.2
  2.2 0.1 stack.13
  2.3 0.6 copy-done.2
  2.9 0.0 copy-start.1
  2.9 0.7 copy-done.1
  3.6 0.1 negate_convert_fusion
  3.6 0.7 maximum_maximum_fusion.steer_ref
  4.3 0.7 fusion.4.table_ref
  5.0 2.6 %reshape.43 = bf16[2,32,2,2,2048]{4,3,2,1,0:T(2,128)(2,1)S(1)} reshape(bf16[2,32,4,2048]{3,2,1,0:T(4,128)(2,1)} %param.10) | data formatting | bytes 2097152 | tf_op jit(solution)/shard_map/reshape | solution.py:659
  7.6 0.8 copy.16
  8.4 1.2 %reshape.44.echo_ref = bf16[2,2,64,2048]{3,2,1,0:T(8,128)(2,1)} reshape(bf16[2,2,32,2,2048]{4,3,2,1,0:T(2,128)(2,1)S(1)} %bitcast.9) | data formatting | bytes 2097152 | tf_op jit(solution)/shard_map/reshape | solution.py:660
  9.6 95.4 %shard_map.100 = bf16[8,32,2048]{2,1,0:T(8,128)(2,1)} custom-call(s32[2,32]{1,0:T(2,128)} %shift_ref.1, f32[3,64]{1,0:T(4,128)} %pad_maximum_fusion.coef_ref, s32[1,16]{1,0:T(1,128)} %foot_ref.1, bf16[2,2,64,2048]{3,2,1,0:T(8,128)(2,1)} %reshape.44.echo_ref, bf16[2,2048]{1,0:T(2,128)(2,1)} %replica_ref.1, bf16[32,32]{1,0:T(8,128)(2,1)} %maximum_maximum_fusion.steer_ref, ...), custom_call_target="tpu_custom_call" | custom-call | tf_op jit(solution)/shard_map/pallas_call | solution.py:594
  105.0 2.3 %copy.18 = bf16[2,4,32,2048]{3,2,1,0:T(8,128)(2,1)} copy(bf16[2,4,32,2048]{3,2,1,0:T(8,128)(2,1)} %bitcast.10) | data formatting | bytes 2097152
  (5 shorter events, 0.1 us)
Async XLA Ops:
  0.0 0.7 copy-start.4
  0.7 0.7 copy-start.5
  0.7 0.7 copy-start.3
  1.3 0.8 copy-start
  2.2 0.7 copy-start.2
  2.9 0.7 copy-start.1

commit v3 on v2

--- a/solution.py
+++ b/solution.py
@@ -201,7 +201,7 @@
     tiles, shift_ref, coef_ref, foot_ref,
     echo_ref, replica_ref, steer_ref, table_ref, out_ref,
     ext_ref, toep_ref, sub_ref, merged_ref, block_ref, kid_ref, tab_ref,
-    kids, tabs, left_ref, part_ref, arrived_ref, own_ref,
+    kids, tabs, packed_ref, left_ref, part_ref, arrived_ref, own_ref,
     halo_send, halo_recv,
     a2a_send, a2a_recv, line_send, line_recv, part_send, part_recv,
 ):
@@ -402,7 +402,7 @@
     def spread_copy(k, d, peer, place):
         if k == CHUNKS:
             src = tab_ref.at[pl.ds(peer * CAP, CAP)]
-            dst = tabs.at[g, pl.ds(place * CAP, CAP)]
+            dst = tabs.at[pl.ds(place * CAP, CAP)]
         else:
             src = kid_ref.at[pl.ds(k * per, per), pl.ds(peer * CAP, CAP)]
             dst = kids.at[g, pl.ds(k * per, per), pl.ds(place * CAP, CAP)]
@@ -425,7 +425,7 @@
 
     def line_copy(k, group, lane, to):
         if k == CHUNKS:
-            part = tabs.at[group]
+            part = packed_ref.at[group]
         else:
             part = kids.at[group, pl.ds(k * per, per)]
         return pltpu.make_async_remote_copy(
@@ -434,11 +434,13 @@
             device_id={"pulse": to}, device_id_type=MESH,
         )
 
-    def part_copy(k, to):
+    middle = spans // 2 * RBLOCK
+
+    def part_copy(k, half, to):
         return pltpu.make_async_remote_copy(
-            src_ref=part_ref.at[pl.ds(k * per, per)],
-            dst_ref=arrived_ref.at[pl.ds(k * per, per)],
-            send_sem=part_send.at[k], recv_sem=part_recv.at[k],
+            src_ref=part_ref.at[pl.ds(k * per, per), :, pl.ds(half * middle, middle)],
+            dst_ref=arrived_ref.at[pl.ds(k * per, per), :, pl.ds(half * middle, middle)],
+            send_sem=part_send.at[k, half], recv_sem=part_recv.at[k, half],
             device_id={"pulse": to}, device_id_type=MESH,
         )
 
@@ -450,33 +452,38 @@
         where_at = (iota((1, lanes), 1) // beams + 1).astype(f32)
         child = iota((32, lanes), 0).astype(f32)
 
-        def four(at, carry):
+        wide = jnp.dot(packed_ref[group], expand, preferred_element_type=f32)
+        for at in range(slots // 4):
             pieces = []
-            for step in range(4):
-                wide = jnp.dot(
-                    tabs[group, at * 4 + step], expand, preferred_element_type=f32
+            for slot in range(at * 4, at * 4 + 4):
+                landing = wide[2 * slots + slot : 2 * slots + slot + 1, :]
+                index = jnp.where(
+                    (landing == where_at) & used, wide[slot : slot + 1, :], -9.0
                 )
-                index = jnp.where((wide[2:3, :] == where_at) & used, wide[0:1, :], -9.0)
-                frac = wide[1:2, :]
+                frac = wide[slots + slot : slots + slot + 1, :]
                 lower = (1.0 - frac).astype(bf16).astype(f32)
                 weight = jnp.where(child == index, lower, 0.0)
                 pieces.append(jnp.where(child == index + 1.0, frac, weight))
             block = jnp.concatenate(pieces, axis=0)
             at_column = pl.multiple_of(column + at * 128, 128)
             left_ref[row : row + lanes, pl.ds(at_column, 128)] = block.T.astype(bf16)
-            return carry
-
-        lax.fori_loop(0, slots // 4, four, 0)
 
     def keep(k):
         if k == CHUNKS:
-            tabs[g, pl.ds(t * CAP, CAP)] = tab_ref[pl.ds(t * CAP, CAP)]
+            tabs[pl.ds(t * CAP, CAP)] = tab_ref[pl.ds(t * CAP, CAP)]
         else:
             span = slice(k * per, (k + 1) * per)
             kids[g, span, pl.ds(t * CAP, CAP)] = kid_ref[span, pl.ds(t * CAP, CAP)]
 
     def begin_own(k):
         spread_wait(k)
+        if k == CHUNKS:
+            row, column = iota((3 * slots, slots * TABROWS), 0), iota((3 * slots, slots * TABROWS), 1)
+            choose = column == (row & (slots - 1)) * TABROWS + row // slots
+            packed_ref[g] = jnp.dot(
+                choose.astype(bf16), tabs[...].reshape(slots * TABROWS, RBLOCK),
+                preferred_element_type=f32,
+            ).astype(bf16)
         line_copy(k, g, 0, inner).start()
 
     spread_start(CHUNKS)
@@ -526,15 +533,18 @@
             right = jnp.concatenate(
                 [kids[:, k * per + i].reshape(4 * depth, RBLOCK) for i in range(per)], axis=1
             )
-            result = jnp.dot(
-                left_ref[lanes:, :], right, preferred_element_type=f32
-            ).astype(bf16)
-            for w in range(spans):
-                for i in range(per):
-                    part_ref[k * per + i, :, w * RBLOCK : (w + 1) * RBLOCK] = result[
-                        w * beams : (w + 1) * beams, i * RBLOCK : (i + 1) * RBLOCK
-                    ]
-            part_copy(k, end).start()
+            for half in range(2):
+                first = lanes + half * (lanes // 2)
+                result = jnp.dot(
+                    left_ref[first : first + lanes // 2, :], right, preferred_element_type=f32
+                ).astype(bf16)
+                for step in range(spans // 2):
+                    w = half * (spans // 2) + step
+                    for i in range(per):
+                        part_ref[k * per + i, :, w * RBLOCK : (w + 1) * RBLOCK] = result[
+                            step * beams : (step + 1) * beams, i * RBLOCK : (i + 1) * RBLOCK
+                        ]
+                part_copy(k, half, end).start()
             result = jnp.dot(
                 left_ref[:lanes, :], right, preferred_element_type=f32
             ).astype(bf16)
@@ -547,7 +557,8 @@
             line_copy(k, g, 0, inner).wait_send()
             line_copy(k, end, 1, inner).wait_send()
         for k in range(CHUNKS):
-            part_copy(k, end).wait_send()
+            for half in range(2):
+                part_copy(k, half, end).wait_send()
 
     @pl.when(jnp.logical_not(is_mid))
     def _():
@@ -567,10 +578,14 @@
                         w * beams : (w + 1) * beams, i * RBLOCK : (i + 1) * RBLOCK
                     ]
         for k in range(CHUNKS):
-            part_copy(k, inner).wait_recv()
-            for i in range(per):
-                x = k * per + i
-                out_ref[i * 4 + k] = (own_ref[x] + arrived_ref[x].astype(f32)).astype(bf16)
+            for half in range(2):
+                part_copy(k, half, inner).wait_recv()
+                span = slice(half * middle, (half + 1) * middle)
+                for i in range(per):
+                    x = k * per + i
+                    out_ref[i * 4 + k, :, span] = (
+                        own_ref[x, :, span] + arrived_ref[x, :, span].astype(f32)
+                    ).astype(bf16)
         for k in order:
             line_copy(k, g, 0, inner).wait_send()
 
@@ -605,7 +620,8 @@
             pltpu.VMEM((8, slots, 32, RBLOCK), bf16),
             pltpu.VMEM((slots, TABROWS, RBLOCK), bf16),
             pltpu.VMEM((4, 8, slots, 32, RBLOCK), bf16),
-            pltpu.VMEM((4, slots, TABROWS, RBLOCK), bf16),
+            pltpu.VMEM((slots, TABROWS, RBLOCK), bf16),
+            pltpu.VMEM((4, 3 * slots, RBLOCK), bf16),
             pltpu.VMEM((2 * lanes, 4 * slots * 32), bf16),
             pltpu.VMEM((8, beams, range_dev), bf16),
             pltpu.VMEM((8, beams, range_dev), bf16),
@@ -616,8 +632,8 @@
             dma((CHUNKS + 1, tiles - 1)),
             dma((2, CHUNKS + 1)),
             dma((4, CHUNKS + 1)),
-            dma((CHUNKS,)),
-            dma((CHUNKS,)),
+            dma((CHUNKS, 2)),
+            dma((CHUNKS, 2)),
         ],
         compiler_params=pltpu.CompilerParams(
             collective_id=0, has_side_effects=True, vmem_limit_bytes=56 << 20

time: 108 us -> 102 us (0.944)
  Pallas kernels: 95.4 us -> 89.8 us
    pallas_call x1, Pallas kernels: 95.4 us -> 89.8 us  [fused(): pl.pallas_call(functools.partial(fused_kernel, tiles), out_shape=jax.Shap...]
where the time goes in v3:
time: 102 us
  Pallas kernels  89.8 us (88%)
  local copies, waits for them, and re-layouts  9.8 us (10%)
  other arithmetic  2.04 us (2%)
    pallas_call x1, Pallas kernels, fused(): pl.pallas_call(functools.partial(fused_kernel, tiles), out_shape=jax.Shap...  89.8 us
    unnamed x13, local copies, waits for them, and re-layouts  4.87 us
    reshape x2, local copies, waits for them, and re-layouts, shards(): echoes.reshape(2, pulse_count, STAGES, pol_count // STAGES, range_dev)  3.37 us

profile of v3, /device:TPU:0, one launch (start us, length us, event | category | flops | bytes accessed | tf_op | source)
XLA Modules:
  0.0 101.7 jit_solution(6007442897633287398)
XLA Ops:
  0.0 0.0 copy-start.4
  0.0 0.7 copy-done.4
  0.7 0.0 copy-start.5
  0.7 0.0 copy-start.3
  0.7 0.1 stack_reshape.9
  0.8 0.6 copy-done.5
  1.3 0.0 copy-start
  1.3 0.0 copy-done.3
  1.4 0.1 stack_reshape.10
  1.5 0.1 stack_reshape.11
  1.6 0.6 pad_maximum_fusion.coef_ref
  2.2 0.0 copy-done
  2.2 0.0 copy-start.2
  2.2 0.1 stack.13
  2.3 0.6 copy-done.2
  2.9 0.0 copy-start.1
  2.9 0.7 copy-done.1
  3.6 0.1 negate_convert_fusion
  3.6 0.7 maximum_maximum_fusion.steer_ref
  4.3 0.7 fusion.4.table_ref
  5.0 2.6 %reshape.43 = bf16[2,32,2,2,2048]{4,3,2,1,0:T(2,128)(2,1)S(1)} reshape(bf16[2,32,4,2048]{3,2,1,0:T(4,128)(2,1)} %param.10) | data formatting | bytes 2097152 | tf_op jit(solution)/shard_map/reshape | solution.py:675
  7.6 0.8 copy.16
  8.4 1.2 %reshape.44.echo_ref = bf16[2,2,64,2048]{3,2,1,0:T(8,128)(2,1)} reshape(bf16[2,2,32,2,2048]{4,3,2,1,0:T(2,128)(2,1)S(1)} %bitcast.9) | data formatting | bytes 2097152 | tf_op jit(solution)/shard_map/reshape | solution.py:676
  9.6 89.8 %shard_map.100 = bf16[8,32,2048]{2,1,0:T(8,128)(2,1)} custom-call(s32[2,32]{1,0:T(2,128)} %shift_ref.1, f32[3,64]{1,0:T(4,128)} %pad_maximum_fusion.coef_ref, s32[1,16]{1,0:T(1,128)} %foot_ref.1, bf16[2,2,64,2048]{3,2,1,0:T(8,128)(2,1)} %reshape.44.echo_ref, bf16[2,2048]{1,0:T(2,128)(2,1)} %replica_ref.1, bf16[32,32]{1,0:T(8,128)(2,1)} %maximum_maximum_fusion.steer_ref, ...), custom_call_target="tpu_custom_call" | custom-call | tf_op jit(solution)/shard_map/pallas_call | solution.py:609
  99.4 2.3 %copy.18 = bf16[2,4,32,2048]{3,2,1,0:T(8,128)(2,1)} copy(bf16[2,4,32,2048]{3,2,1,0:T(8,128)(2,1)} %bitcast.10) | data formatting | bytes 2097152
  (5 shorter events, 0.1 us)
Async XLA Ops:
  0.0 0.7 copy-start.4
  0.7 0.7 copy-start.5
  0.7 0.7 copy-start.3
  1.3 0.8 copy-start
  2.2 0.7 copy-start.2
  2.9 0.7 copy-start.1

commit v4 on v3

--- a/solution.py
+++ b/solution.py
@@ -190,7 +190,7 @@
                 ]
 
 
-CHUNKS = 4
+CHUNKS = 8
 MESH = pl.DeviceIdType.MESH
 
 
@@ -213,6 +213,10 @@
     slots = tiles * CAP
     depth = slots * 32
     per = 8 // CHUNKS
+
+    def out_at(x):
+        return (x % 2) * 4 + x // 2
+
     bf16 = jnp.bfloat16
     f32 = jnp.float32
     is_mid = (g == 1) | (g == 2)
@@ -252,7 +256,7 @@
     def halo_copy(stage, j):
         (first, count), to, by = halos[j]
         return pltpu.make_async_remote_copy(
-            src_ref=echo_ref.at[stage, :, :, pl.ds(first, count)],
+            src_ref=echo_ref.at[:, stage, :, pl.ds(first, count)],
             dst_ref=ext_ref.at[stage, :, :, pl.ds(to, count)],
             send_sem=halo_send.at[stage, j], recv_sem=halo_recv.at[stage, j],
             device_id={"tile": lax.rem(t + by + tiles, tiles)}, device_id_type=MESH,
@@ -280,7 +284,7 @@
             def _():
                 ext_ref[stage, :, :, to : to + count] = jnp.zeros((2, rows, count), bf16)
 
-        ext_ref[stage, :, :, EDGE : EDGE + range_dev] = echo_ref[stage]
+        ext_ref[stage, :, :, EDGE : EDGE + range_dev] = echo_ref[:, stage]
 
     for part in range(2):
         line = replica_ref[part : part + 1, :].astype(f32)
@@ -301,11 +305,11 @@
     left = ((picked * 16 + ((r_at >> 3) & 15)) == iota((256, 32), 1)).astype(f32)
     left = jnp.where((turn == 1) & (want == 0), -left, left).astype(bf16)
     k_at = iota((32, 128), 1)
-    right = ((k_at >> 6) * 16 + ((k_at >> 1) & 15) == iota((32, 128), 0)).astype(bf16)
+    right = ((k_at >> 6) * 16 + (k_at & 15) == iota((32, 128), 0)).astype(bf16)
     spread = jnp.dot(left, steer_ref[...], preferred_element_type=f32).astype(bf16)
     spread = jnp.dot(spread, right, preferred_element_type=f32)
     r_all, k_all = iota((256, 128), 0), iota((256, 128), 1)
-    same = ((r_all >> 7) == ((k_all >> 5) & 1)) & ((r_all & 1) == (k_all & 1))
+    same = ((r_all >> 7) == ((k_all >> 4) & 1)) & ((r_all & 1) == ((k_all >> 5) & 1))
     steer = jnp.where(same, spread, 0.0).astype(bf16)
     o_all, i_all = iota((128, 128), 0), iota((128, 128), 1)
     order_in = (o_all & 31) * 4 + ((o_all >> 5) & 1) * 2 + (o_all >> 6)
@@ -489,16 +493,16 @@
     spread_start(CHUNKS)
     keep(CHUNKS)
     form(0, lambda: begin_own(CHUNKS))
-    for k in (0, 1):
+    for k in range(CHUNKS // 2):
         spread_start(k)
         keep(k)
 
     def between():
-        begin_own(0)
-        begin_own(1)
+        for k in range(CHUNKS // 2):
+            begin_own(k)
 
     form(1, between)
-    for k in (2, 3):
+    for k in range(CHUNKS // 2, CHUNKS):
         spread_start(k)
         keep(k)
 
@@ -523,11 +527,12 @@
             return carry
 
         lax.fori_loop(0, 4, prepare_group, 0)
-        relay(1)
-        begin_own(2)
-        begin_own(3)
+        for k in range(1, CHUNKS // 2):
+            relay(k)
+        for k in range(CHUNKS // 2, CHUNKS):
+            begin_own(k)
         for k in range(CHUNKS):
-            if 2 <= k + 1 < CHUNKS:
+            if CHUNKS // 2 <= k + 1 < CHUNKS:
                 relay(k + 1)
             finish(k)
             right = jnp.concatenate(
@@ -550,7 +555,7 @@
             ).astype(bf16)
             for w in range(spans):
                 for i in range(per):
-                    out_ref[i * 4 + k, :, w * RBLOCK : (w + 1) * RBLOCK] = result[
+                    out_ref[out_at(k * per + i), :, w * RBLOCK : (w + 1) * RBLOCK] = result[
                         w * beams : (w + 1) * beams, i * RBLOCK : (i + 1) * RBLOCK
                     ]
         for k in order:
@@ -562,8 +567,8 @@
 
     @pl.when(jnp.logical_not(is_mid))
     def _():
-        begin_own(2)
-        begin_own(3)
+        for k in range(CHUNKS // 2, CHUNKS):
+            begin_own(k)
         prepare(g, g, 0, 0, g >= 0)
         for k in range(CHUNKS):
             right = jnp.concatenate(
@@ -583,7 +588,7 @@
                 span = slice(half * middle, (half + 1) * middle)
                 for i in range(per):
                     x = k * per + i
-                    out_ref[i * 4 + k, :, span] = (
+                    out_ref[out_at(x), :, span] = (
                         own_ref[x, :, span] + arrived_ref[x, :, span].astype(f32)
                     ).astype(bf16)
         for k in order:
@@ -612,7 +617,7 @@
         in_specs=[smem] * 3 + [vmem] * 4,
         out_specs=vmem,
         scratch_shapes=[
-            pltpu.VMEM(echoes.shape[:3] + (2 * range_dev + 2 * EDGE,), bf16),
+            pltpu.VMEM((STAGES, 2, echoes.shape[2], 2 * range_dev + 2 * EDGE), bf16),
             pltpu.VMEM((2 * CBLOCK, 2 * (CBLOCK + replica.shape[1])), bf16),
             pltpu.VMEM((256, range_dev + CBLOCK), jnp.float32),
             pltpu.VMEM((128, range_dev), jnp.float32),
@@ -672,8 +677,7 @@
     )
     beams = final_beams // groups
     if groups == 4 and slot_count == range_dev // RBLOCK:
-        split = echoes.reshape(2, pulse_count, STAGES, pol_count // STAGES, range_dev)
-        split = split.transpose(2, 0, 1, 3, 4).reshape(STAGES, 2, rows // STAGES, range_dev)
+        split = echoes.transpose(0, 2, 1, 3).reshape(2, STAGES, rows // STAGES, range_dev)
         landing = jnp.broadcast_to(row_slot[0][:, None] + 1, beam_index.shape[1:])
         tables = jnp.stack(
             [beam_index[0].astype(jnp.float32), beam_frac[0].astype(jnp.float32),

time: 102 us -> 101 us (level)
  local copies, waits for them, and re-layouts: 9.8 us -> 7.99 us
  Pallas kernels: 89.8 us -> 91.1 us
    reshape x3 -> x0, local copies, waits for them, and re-layouts: 4.59 us -> none  [the longest x2 3.37 us: shards(): echoes.reshape(2, pulse_count, STAGES, pol_count // STAGES, range_dev)]
    transpose x0 -> x1, local copies, waits for them, and re-layouts: none -> 2.77 us  [shards(): echoes.transpose(0, 2, 1, 3).reshape(2, STAGES, rows // STAGES, range_dev)]
    pallas_call x1, Pallas kernels: 89.8 us -> 91.1 us  [fused(): pl.pallas_call(functools.partial(fused_kernel, tiles), out_shape=jax.Shap...]
where the time goes in v4:
time: 101 us
  Pallas kernels  91.1 us (90%)
  local copies, waits for them, and re-layouts  7.99 us (8%)
  other arithmetic  2.04 us (2%)
    pallas_call x1, Pallas kernels, fused(): pl.pallas_call(functools.partial(fused_kernel, tiles), out_shape=jax.Shap...  91.1 us
    unnamed x13, local copies, waits for them, and re-layouts  4.87 us
    transpose x1, local copies, waits for them, and re-layouts, shards(): echoes.transpose(0, 2, 1, 3).reshape(2, STAGES, rows // STAGES, range_dev)  2.77 us

profile of v4, /device:TPU:0, one launch (start us, length us, event | category | flops | bytes accessed | tf_op | source)
XLA Modules:
  0.0 101.2 jit_solution(11666783745797729795)
XLA Ops:
  0.0 0.0 copy-start.4
  0.0 0.7 copy-done.4
  0.7 0.0 copy-start.5
  0.7 0.0 copy-start.3
  0.7 0.1 stack_reshape.9
  0.8 0.6 copy-done.5
  1.3 0.0 copy-start
  1.3 0.0 copy-done.3
  1.4 0.1 stack_reshape.10
  1.5 0.1 stack_reshape.11
  1.6 0.6 pad_maximum_fusion.coef_ref
  2.2 0.0 copy-done
  2.2 0.0 copy-start.2
  2.2 0.1 stack.13
  2.3 0.6 copy-done.2
  2.9 0.0 copy-start.1
  2.9 0.7 copy-done.1
  3.6 0.1 negate_convert_fusion
  3.6 0.7 maximum_maximum_fusion.steer_ref
  4.3 0.7 fusion.4.table_ref
  5.0 2.8 %copy.12 = bf16[2,4,32,2048]{3,2,1,0:T(8,128)(2,1)} copy(bf16[2,4,32,2048]{3,1,2,0:T(4,128)(2,1)} %bitcast.10) | data formatting | bytes 2097152 | tf_op jit(solution)/shard_map/transpose | solution.py:680
  7.8 91.1 %shard_map.100 = bf16[8,32,2048]{2,1,0:T(8,128)(2,1)} custom-call(s32[2,32]{1,0:T(2,128)} %shift_ref.1, f32[3,64]{1,0:T(4,128)} %pad_maximum_fusion.coef_ref, s32[1,16]{1,0:T(1,128)} %foot_ref.1, bf16[2,2,64,2048]{3,2,1,0:T(8,128)(2,1)} %bitcast.9, bf16[2,2048]{1,0:T(2,128)(2,1)} %replica_ref.1, bf16[32,32]{1,0:T(8,128)(2,1)} %maximum_maximum_fusion.steer_ref, ...), custom_call_target="tpu_custom_call" | custom-call | tf_op jit(solution)/shard_map/pallas_call | solution.py:614
  98.9 2.3 %copy.16 = bf16[2,4,32,2048]{3,2,1,0:T(8,128)(2,1)} copy(bf16[2,4,32,2048]{3,2,1,0:T(8,128)(2,1)} %bitcast.8) | data formatting | bytes 2097152
  (5 shorter events, 0.1 us)
Async XLA Ops:
  0.0 0.7 copy-start.4
  0.7 0.7 copy-start.5
  0.7 0.7 copy-start.3
  1.3 0.8 copy-start
  2.2 0.7 copy-start.2
  2.9 0.7 copy-start.1
